TPU v7x, 256 devices: a whole 4x4x8 slice. The times are simulated.
256 devices in a mesh: child: 2 (over core), row: 4 (over x), col: 32 (over y, z).
Axes of the slice: x: 4, y: 4, z: 8, core: 2. Of those that a mesh axis runs over, the one named last changes fastest.
Arguments:
- schur_blocks: bfloat16 [2, 16384, 16384], P('child', 'row', 'col'), may hold values from -2 to 2
- child_map: int32 [2, 16384], replicated, may hold values from 0 to 24575, as said below
- round_seeds: int32 [2], replicated, may hold values from 1 to 999999
Outputs:
- leaf_bases: float32 [24576, 256], P(('row', 'child', 'col'))
- fresh_samples: float32 [24576, 256], P(('row', 'child', 'col'))
Inputs may be any that keep to these rules, and one draw needn't show every extreme that they name: For each child c and each block r < 4, the entries child_map[c, r * 4096 : (r + 1) * 4096] rise strictly, lie in parent rows [r * 6144, (r + 1) * 6144), and include both ends of that range.
All inputs are finite; a program needn't handle non-finite values.
Results may differ from a plain program's by a relative error of at most 0.0031.
Values sent between devices are 32-bit elements; how exact they have to be, the bound alone decides.
A program may use at most 64 MiB of HBM per device.

v0:
```python
import jax
import jax.numpy as jnp
from jax import lax
from jax.sharding import PartitionSpec as P

NP = 24576
K = 256


def sample_rows(seed_value, parents, sample_width):
    hashed = (
        parents[:, None] * 40503
        + lax.iota(jnp.int32, sample_width)[None, :] * 9973
        + seed_value * 2654435
    )
    hashed = hashed ^ hashed >> 15 & 131071
    hashed = hashed * 73244475
    hashed = hashed ^ hashed >> 13 & 524287
    hashed = hashed * 1274126177
    hashed = hashed ^ hashed >> 16 & 65535
    unit_value = (hashed & 16777215).astype(jnp.float32) * (1.0 / 16777216.0)
    return (unit_value - 0.5) * 3.4641016


def body(schur_blocks, child_map, round_seeds):
    child_block = schur_blocks[0]
    block_rows, block_cols = child_block.shape
    child_count = lax.axis_size("child")
    col_count = lax.axis_size("col")
    row_count_axis = lax.axis_size("row")
    child_index = lax.axis_index("child")
    row_index = lax.axis_index("row")
    col_index = lax.axis_index("col")
    child_order = child_map.shape[1]
    own_map = lax.dynamic_index_in_dim(child_map, child_index, 0, keepdims=False)
    col_ids = lax.dynamic_slice_in_dim(own_map, col_index * block_cols, block_cols)
    leaf_rows = NP // row_count_axis
    own_rows = leaf_rows // (child_count * col_count)
    leaf_base = row_index * leaf_rows

    def sketch_rows(seed_list):
        samples = jnp.concatenate(
            [sample_rows(seed_value, col_ids, K) for seed_value in seed_list], axis=1
        ).astype(jnp.bfloat16)
        return jnp.dot(child_block, samples, preferred_element_type=jnp.float32)

    def extend(partial_value):
        summed = lax.psum_scatter(partial_value, "col", scatter_dimension=0, tiled=True)
        flat_map = child_map.reshape(-1)
        wanted = (
            leaf_base
            + (child_index * col_count + col_index) * own_rows
            + lax.iota(jnp.int32, own_rows)
        )
        shard_rows = lax.all_gather(summed, ("child", "col"), axis=0, tiled=True)
        gathered_pos = lax.iota(jnp.int32, shard_rows.shape[0])
        source = (
            gathered_pos // block_rows * child_order
            + row_index * block_rows
            + gathered_pos % block_rows
        )
        parent_ids = jnp.take(flat_map, source)
        select = (wanted[:, None] == parent_ids[None, :]).astype(jnp.float32)
        return jnp.dot(select, shard_rows, precision=lax.Precision.HIGHEST)

    first_leaf = extend(sketch_rows([round_seeds[0]]))
    second_leaf = extend(sketch_rows([round_seeds[1]]))
    gram_local = jnp.dot(first_leaf.T, first_leaf, precision=lax.Precision.HIGHEST)
    gram_matrix = lax.psum(gram_local, ("child", "col")) / leaf_rows
    lower_factor = jnp.linalg.cholesky(gram_matrix)
    leaf_basis = lax.linalg.triangular_solve(
        lower_factor, first_leaf, left_side=False, lower=True, transpose_a=True
    )
    coef_local = jnp.dot(leaf_basis.T, second_leaf, precision=lax.Precision.HIGHEST)
    coefficients = lax.psum(coef_local, ("child", "col")) / leaf_rows
    fresh_samples = second_leaf - jnp.dot(leaf_basis, coefficients, precision=lax.Precision.HIGHEST)
    return (leaf_basis, fresh_samples)


def solution(mesh):
    placed = (P("child", "row", "col"), P(), P())
    return jax.shard_map(
        body,
        mesh=mesh,
        in_specs=placed,
        out_specs=(P(("row", "child", "col"), None), P(("row", "child", "col"), None)),
        check_vma=False,
    )
```

profile of v0, /device:TPU:1, one launch (start us, length us, event | category | flops | bytes accessed | tf_op | source)
XLA Modules:
  0.0 1073.4 jit_solution(4717258641060240434)
XLA Ops:
  7.2 1.3 fusion.102
  9.9 5.7 convolution_bitcast_fusion.1
  16.3 5.7 convolution_bitcast_fusion
  22.1 217.3 %reduce-scatter.3.cloned.1.call-done = f32[128,256]{0,1:T(8,128)} async-done(((f32[4096,256]{0,1:T(8,128)}), f32[128,256]{0,1:T(8,128)}) %reduce-scatter.3.cloned.1.call-update) | async-done | bytes 131088 | tf_op jit(solution)/shard_map/reduce_scatter | solution.py:48
  239.6 226.7 %reduce-scatter.5.cloned.1.call-done = f32[128,256]{0,1:T(8,128)} async-done(((f32[4096,256]{0,1:T(8,128)}), f32[128,256]{0,1:T(8,128)}) %reduce-scatter.5.cloned.1.call-update) | async-done | bytes 131088 | tf_op jit(solution)/shard_map/reduce_scatter | solution.py:48
  466.4 45.5 %gather_fusion = s32[8192]{0:T(1024)S(1)} fusion(s32[32768]{0:T(1024)S(1)} %bitcast.52, s32[8192]{0:T(1024)S(1)} %broadcast_clamp_fusion), kind=kCustom, calls=%fused_computation.clone | custom fusion | bytes 98304 | tf_op jit(solution)/shard_map/jit(_take)/gather | solution.py:62
  512.0 45.2 %all-gather.3.cloned.1.call-done = f32[8192,256]{0,1:T(8,128)} async-done(((f32[128,256]{0,1:T(8,128)}), f32[8192,256]{0,1:T(8,128)}) %all-gather.3.cloned.1.call-update) | async-done | bytes 8388624 | tf_op jit(solution)/shard_map/all_gather | solution.py:55
  557.2 8.0 fusion.4
  565.2 1.1 fusion.103
  566.6 78.4 %all-gather.5.cloned.1.call-done = f32[8192,256]{0,1:T(8,128)} async-done(((f32[128,256]{0,1:T(8,128)}), f32[8192,256]{0,1:T(8,128)}) %all-gather.5.cloned.1.call-update) | async-done | bytes 8388624 | tf_op jit(solution)/shard_map/all_gather | solution.py:55
  645.0 8.0 fusion.2
  653.1 173.0 %all-reduce.4.cloned.1.call-done = f32[256,256]{0,1:T(8,128)} async-done(((f32[256,256]{0,1:T(8,128)}), f32[256,256]{0,1:T(8,128)}) %all-reduce.4.cloned.1.call-update) | async-done | bytes 262160 | tf_op jit(solution)/shard_map/psum | solution.py:69
  826.0 1.0 broadcast_multiply_fusion
  827.1 1.0 fusion.26
  828.2 11.7 %cholesky.50 = f32[128,128]{1,0:T(8,128)S(1)} custom-call(f32[128,128]{1,0:T(8,128)S(1)} %cholesky.118), custom_call_target="Cholesky" | custom-call | tf_op jit(solution)/shard_map/jit(cholesky)/cholesky | solution.py:70
  839.9 9.8 custom-call.14
  850.2 11.9 %cholesky.105 = f32[128,128]{1,0:T(8,128)S(1)} custom-call(f32[128,128]{1,0:T(8,128)S(1)} %convolution_subtract_fusion.1), custom_call_target="Cholesky" | custom-call | tf_op jit(solution)/shard_map/jit(cholesky)/cholesky | solution.py:70
  864.2 3.9 while.1
  864.8 1.3 bitcast_dynamic-update-slice_fusion.2
  866.8 1.3 bitcast_dynamic-update-slice_fusion.2
  868.1 19.7 %custom-call.15 = f32[2,128,128]{1,2,0:T(8,128)S(1)} custom-call(f32[2,128,128]{2,1,0:T(8,128)S(1)} %get-tuple-element.10), custom_call_target="InvertDiagBlocksLowerTriangular" | custom-call | tf_op jit(solution)/shard_map/triangular_solve | solution.py:71
  888.5 1.1 fusion.104
  889.6 174.9 %all-reduce.6.cloned.1.call-done = f32[256,256]{0,1:T(8,128)} async-done(((f32[256,256]{0,1:T(8,128)}), f32[256,256]{0,1:T(8,128)}) %all-reduce.6.cloned.1.call-update) | async-done | bytes 262160 | tf_op jit(solution)/shard_map/psum | solution.py:75
  1064.6 2.0 convolution_subtract_fusion
  (42 shorter events, 4.7 us)
Async XLA Ops:
  7.2 232.3 %reduce-scatter.3.cloned.1.call-start = ((), (), s32[]{:S(2)}) async-start(), calls=%async_computation.2 | async-start | bytes 4325376 | tf_op jit(solution)/shard_map/reduce_scatter | solution.py:48
  15.7 450.6 %reduce-scatter.5.cloned.1.call-start = ((), (), s32[]{:S(2)}) async-start(), calls=%async_computation.5 | async-start | bytes 4325376 | tf_op jit(solution)/shard_map/reduce_scatter | solution.py:48
  22.1 444.3 %copy-start.1 = (s32[2,16384]{1,0:T(2,128)S(1)}, s32[2,16384]{1,0:T(2,128)}, u32[]{:S(2)}) copy-start(s32[2,16384]{1,0:T(2,128)} %param.6) | copy-start | bytes 393220
  22.1 535.1 %all-gather.3.cloned.1.call-start = ((), (), s32[]{:S(2)}) async-start(), calls=%async_computation.3 | async-start | bytes 8519680 | tf_op jit(solution)/shard_map/all_gather | solution.py:55
  239.5 405.5 %all-gather.5.cloned.1.call-start = ((), (), s32[]{:S(2)}) async-start(), calls=%async_computation.6 | async-start | bytes 8519680 | tf_op jit(solution)/shard_map/all_gather | solution.py:55
  466.3 359.8 %all-reduce.4.cloned.1.call-start = ((), (), s32[]{:S(2)}) async-start(), calls=%async_computation.4 | async-start | bytes 524288 | tf_op jit(solution)/shard_map/psum | solution.py:69
  566.4 498.2 %all-reduce.6.cloned.1.call-start = ((), (), s32[]{:S(2)}) async-start(), calls=%async_computation.7 | async-start | bytes 524288 | tf_op jit(solution)/shard_map/psum | solution.py:75
  888.5 178.0 %copy-start = (f32[96,256]{1,0:T(8,128)}, f32[96,256]{1,0:T(8,128)S(1)}, u32[]{:S(2)}) copy-start(f32[96,256]{1,0:T(8,128)S(1)} %pad_maximum_fusion) | copy-start | bytes 294916
Sparse Core Ops, SparseCore 0:
  15.8 223.6 reduce-scatter.2
  243.4 222.8 reduce-scatter.4
  468.8 88.3 all-gather.2
  559.6 85.3 all-gather.4
  648.4 177.6 all-reduce.3
  889.8 174.7 all-reduce.5
where the time goes:
time: 1070 us
  waiting for transfers between devices  916 us (86%)
  other arithmetic  56.7 us (5%)
  local copies, waits for them, and re-layouts  51 us (5%)
  matrix products  32.8 us (3%)
  between operations  16.9 us (2%)
    reduce_scatter x2, waiting for transfers between devices, extend(): lax.psum_scatter(partial_value, 'col', scatter_dimension=0, tiled=True)  444 us
    psum x1, waiting for transfers between devices, body(): coefficients = lax.psum(coef_local, ('child', 'col')) / leaf_rows  175 us
    psum x1, waiting for transfers between devices, body(): gram_matrix = lax.psum(gram_local, ('child', 'col')) / leaf_rows  173 us
    all_gather x2, waiting for transfers between devices, extend(): shard_rows = lax.all_gather(summed, ('child', 'col'), axis=0, tiled=True)  124 us
    gather x1, local copies, waits for them, and re-layouts, extend(): parent_ids = jnp.take(flat_map, source)  45.5 us
    another operation x6, other arithmetic, body(): lower_factor = jnp.linalg.cholesky(gram_matrix)  34.2 us
  transfers between devices with their start and end apart: 6, of which 6 were waited for; matrix products, arithmetic and copies ran while one was open for 6% of the time, Pallas kernels for 0%

commit v1 on v0

--- a/solution.py
+++ b/solution.py
@@ -72,7 +72,7 @@
         lower_factor, first_leaf, left_side=False, lower=True, transpose_a=True
     )
     coef_local = jnp.dot(leaf_basis.T, second_leaf, precision=lax.Precision.HIGHEST)
-    coefficients = lax.psum(coef_local, ("child", "col")) / leaf_rows
+    coefficients = jnp.sum(lax.all_gather(coef_local, ("child", "col")), axis=0) / leaf_rows
     fresh_samples = second_leaf - jnp.dot(leaf_basis, coefficients, precision=lax.Precision.HIGHEST)
     return (leaf_basis, fresh_samples)
 

time: 1070 us -> 1000 us (0.935)
  waiting for transfers between devices: 916 us -> 838 us
    psum x1 -> x0, waiting for transfers between devices: 175 us -> none  [body(): coefficients = lax.psum(coef_local, ('child', 'col')) / leaf_rows]
    all_gather x0 -> x1, waiting for transfers between devices: none -> 96.9 us  [body(): lax.all_gather(coef_local, ('child', 'col'))]
  transfers between devices with their start and end apart: 6 -> 6, of which waited for: 6 -> 6; matrix products, arithmetic and copies ran while one was open for 6% -> 7% of each run, Pallas kernels for 0% -> 0%
where the time goes in v1:
time: 1000 us
  waiting for transfers between devices  838 us (84%)
  other arithmetic  63.5 us (6%)
  local copies, waits for them, and re-layouts  51.1 us (5%)
  matrix products  31.8 us (3%)
  between operations  16.9 us (2%)
    reduce_scatter x2, waiting for transfers between devices, extend(): lax.psum_scatter(partial_value, 'col', scatter_dimension=0, tiled=True)  444 us
    psum x1, waiting for transfers between devices, body(): gram_matrix = lax.psum(gram_local, ('child', 'col')) / leaf_rows  173 us
    all_gather x2, waiting for transfers between devices, extend(): shard_rows = lax.all_gather(summed, ('child', 'col'), axis=0, tiled=True)  124 us
    all_gather x1, waiting for transfers between devices, body(): lax.all_gather(coef_local, ('child', 'col'))  96.9 us
    gather x1, local copies, waits for them, and re-layouts, extend(): parent_ids = jnp.take(flat_map, source)  45.5 us
    another operation x6, other arithmetic, body(): lower_factor = jnp.linalg.cholesky(gram_matrix)  34.2 us
  transfers between devices with their start and end apart: 6, of which 6 were waited for; matrix products, arithmetic and copies ran while one was open for 7% of the time, Pallas kernels for 0%

profile of v1, /device:TPU:1, one launch (start us, length us, event | category | flops | bytes accessed | tf_op | source)
XLA Modules:
  0.0 1001.4 jit_solution(10515843386591329316)
XLA Ops:
  7.2 1.3 fusion.102
  9.9 5.7 convolution_bitcast_fusion.1
  16.3 5.7 convolution_bitcast_fusion
  22.1 217.3 %reduce-scatter.3.cloned.1.call-done = f32[128,256]{0,1:T(8,128)} async-done(((f32[4096,256]{0,1:T(8,128)}), f32[128,256]{0,1:T(8,128)}) %reduce-scatter.3.cloned.1.call-update) | async-done | bytes 131088 | tf_op jit(solution)/shard_map/reduce_scatter | solution.py:48
  239.6 226.7 %reduce-scatter.5.cloned.1.call-done = f32[128,256]{0,1:T(8,128)} async-done(((f32[4096,256]{0,1:T(8,128)}), f32[128,256]{0,1:T(8,128)}) %reduce-scatter.5.cloned.1.call-update) | async-done | bytes 131088 | tf_op jit(solution)/shard_map/reduce_scatter | solution.py:48
  466.4 45.5 %gather_fusion = s32[8192]{0:T(1024)S(1)} fusion(s32[32768]{0:T(1024)S(1)} %bitcast.53, s32[8192]{0:T(1024)S(1)} %broadcast_clamp_fusion), kind=kCustom, calls=%fused_computation.clone | custom fusion | bytes 98304 | tf_op jit(solution)/shard_map/jit(_take)/gather | solution.py:62
  512.0 45.2 %all-gather.5.cloned.1.call-done = f32[8192,256]{0,1:T(8,128)} async-done(((f32[128,256]{0,1:T(8,128)}), f32[8192,256]{0,1:T(8,128)}) %all-gather.5.cloned.1.call-update) | async-done | bytes 8388624 | tf_op jit(solution)/shard_map/all_gather | solution.py:55
  557.2 8.0 fusion.4
  565.2 1.1 fusion.103
  566.6 78.4 %all-gather.7.cloned.1.call-done = f32[8192,256]{0,1:T(8,128)} async-done(((f32[128,256]{0,1:T(8,128)}), f32[8192,256]{0,1:T(8,128)}) %all-gather.7.cloned.1.call-update) | async-done | bytes 8388624 | tf_op jit(solution)/shard_map/all_gather | solution.py:55
  645.0 8.0 fusion.2
  653.1 173.0 %all-reduce.3.cloned.1.call-done = f32[256,256]{0,1:T(8,128)} async-done(((f32[256,256]{0,1:T(8,128)}), f32[256,256]{0,1:T(8,128)}) %all-reduce.3.cloned.1.call-update) | async-done | bytes 262160 | tf_op jit(solution)/shard_map/psum | solution.py:69
  827.1 1.0 fusion.26
  828.2 11.7 %cholesky.50 = f32[128,128]{1,0:T(8,128)S(1)} custom-call(f32[128,128]{1,0:T(8,128)S(1)} %cholesky.118), custom_call_target="Cholesky" | custom-call | tf_op jit(solution)/shard_map/jit(cholesky)/cholesky | solution.py:70
  839.9 9.8 custom-call.14
  850.2 11.9 %cholesky.105 = f32[128,128]{1,0:T(8,128)S(1)} custom-call(f32[128,128]{1,0:T(8,128)S(1)} %convolution_subtract_fusion.1), custom_call_target="Cholesky" | custom-call | tf_op jit(solution)/shard_map/jit(cholesky)/cholesky | solution.py:70
  864.2 3.9 while.1
  864.8 1.3 bitcast_dynamic-update-slice_fusion.2
  866.8 1.3 bitcast_dynamic-update-slice_fusion.2
  868.1 19.7 %custom-call.15 = f32[2,128,128]{1,2,0:T(8,128)S(1)} custom-call(f32[2,128,128]{2,1,0:T(8,128)S(1)} %get-tuple-element.10), custom_call_target="InvertDiagBlocksLowerTriangular" | custom-call | tf_op jit(solution)/shard_map/triangular_solve | solution.py:71
  888.5 1.1 fusion.104
  889.7 96.9 %all-gather.9.cloned.1.call-done = f32[16384,256]{1,0:T(8,128)} async-done(((f32[256,256]{1,0:T(8,128)}), f32[16384,256]{1,0:T(8,128)}) %all-gather.9.cloned.1.call-update) | async-done | bytes 16777232 | tf_op jit(solution)/shard_map/all_gather | solution.py:75
  986.5 6.8 reduce_sum.9
  993.5 1.0 convolution_subtract_fusion
  (44 shorter events, 5.8 us)
Async XLA Ops:
  7.2 232.3 %reduce-scatter.3.cloned.1.call-start = ((), (), s32[]{:S(2)}) async-start(), calls=%async_computation.2 | async-start | bytes 4325376 | tf_op jit(solution)/shard_map/reduce_scatter | solution.py:48
  15.7 450.6 %reduce-scatter.5.cloned.1.call-start = ((), (), s32[]{:S(2)}) async-start(), calls=%async_computation.5 | async-start | bytes 4325376 | tf_op jit(solution)/shard_map/reduce_scatter | solution.py:48
  22.1 444.3 %copy-start.1 = (s32[2,16384]{1,0:T(2,128)S(1)}, s32[2,16384]{1,0:T(2,128)}, u32[]{:S(2)}) copy-start(s32[2,16384]{1,0:T(2,128)} %param.6) | copy-start | bytes 393220
  22.1 535.1 %all-gather.5.cloned.1.call-start = ((), (), s32[]{:S(2)}) async-start(), calls=%async_computation.3 | async-start | bytes 8519680 | tf_op jit(solution)/shard_map/all_gather | solution.py:55
  239.5 405.5 %all-gather.7.cloned.1.call-start = ((), (), s32[]{:S(2)}) async-start(), calls=%async_computation.6 | async-start | bytes 8519680 | tf_op jit(solution)/shard_map/all_gather | solution.py:55
  466.3 359.8 %all-reduce.3.cloned.1.call-start = ((), (), s32[]{:S(2)}) async-start(), calls=%async_computation.4 | async-start | bytes 524288 | tf_op jit(solution)/shard_map/psum | solution.py:69
  566.4 420.2 %all-gather.9.cloned.1.call-start = ((), (), s32[]{:S(2)}) async-start(), calls=%async_computation.7 | async-start | bytes 17039360 | tf_op jit(solution)/shard_map/all_gather | solution.py:75
  888.5 105.0 %copy-start = (f32[96,256]{1,0:T(8,128)}, f32[96,256]{1,0:T(8,128)S(1)}, u32[]{:S(2)}) copy-start(f32[96,256]{1,0:T(8,128)S(1)} %pad_maximum_fusion) | copy-start | bytes 294916
Sparse Core Ops, SparseCore 0:
  15.8 223.6 reduce-scatter.2
  243.4 222.8 reduce-scatter.4
  468.8 88.3 all-gather.4
  559.6 85.3 all-gather.6
  648.4 177.6 all-reduce.2
  889.8 96.7 all-gather.8
